TPU v7x, 32 devices: a whole 2x2x4 slice. The times are simulated.
32 devices in a mesh: seq: 8 (over y, x, core), tp: 4 (over z).
Axes of the slice: x: 2, y: 2, z: 4, core: 2. Of those that a mesh axis runs over, the one named last changes fastest.
Arguments:
- layer_in: bfloat16 [2, 2048, 2048], P(None, 'seq'), may hold values from -6 to 6
- attn_gain: float32 [2048], replicated, may hold values from 0.1 to 1.9
- query_down: bfloat16 [2048, 1024], replicated, may hold values from -0.125 to 0.125
- latent_gain: float32 [1024], replicated, may hold values from 0.1 to 1.9
- query_up: bfloat16 [1024, 4096], P(None, 'tp'), may hold values from -0.1875 to 0.1875
- key_value: bfloat16 [2048, 512], replicated, may hold values from -0.125 to 0.125
- attn_out: bfloat16 [4096, 2048], P('tp'), may hold values from -1.5 to 1.5
- ffn_gain: float32 [2048], replicated, may hold values from 0.1 to 1.9
- gate_proj: bfloat16 [2048, 5632], P(None, 'tp'), may hold values from -0.125 to 0.125
- up_proj: bfloat16 [2048, 5632], P(None, 'tp'), may hold values from -0.125 to 0.125
- down_proj: bfloat16 [5632, 2048], P('tp'), may hold values from -0.078125 to 0.078125
- out_grad: bfloat16 [2, 2048, 2048], P(None, 'seq'), may hold values from -6 to 6
- doc_lengths: int32 [2, 8], replicated, may hold values from 1 to 1536, 2048 in all within a row
Outputs:
- layer_out: bfloat16 [2, 2048, 2048], P(None, 'seq')
- input_grad: bfloat16 [2, 2048, 2048], P(None, 'seq')
- attn_gain_grad: float32 [2048], P('seq')
- query_down_grad: float32 [2048, 1024], P('seq')
- latent_gain_grad: float32 [1024], P('seq')
- query_up_grad: float32 [1024, 4096], P('seq', 'tp')
- key_value_grad: float32 [2048, 512], P('seq')
- attn_out_grad: float32 [4096, 2048], P('tp', 'seq')
- ffn_gain_grad: float32 [2048], P('seq')
- gate_proj_grad: float32 [2048, 5632], P('seq', 'tp')
- up_proj_grad: float32 [2048, 5632], P('seq', 'tp')
- down_proj_grad: float32 [5632, 2048], P('tp', 'seq')
Inputs may be any that keep to these rules, and one draw needn't show every extreme that they name: `doc_lengths`: in each row the 8 lengths add up to 2048, and the longest is exactly 1536.
All inputs are finite; a program needn't handle non-finite values.
Results may differ from a plain program's by a relative error of at most 0.019.
Values may be sent and summed in bfloat16 or wider, within the bound.
No kernel may reach another device: no remote copies, remote signals or barrier semaphores. Data moves between devices by JAX's collectives and lax.ppermute only.
A program may use at most 256 MiB of HBM per device.

v0:
```python
import jax
import jax.numpy as jnp
from jax import lax
from jax.sharding import PartitionSpec as P

HD = 256
EPS = 1e-05
ROPE_BASE = 10000.0
NEG_FILL = -1e30


def matmul(left, right):
    return jnp.dot(left, right, preferred_element_type=jnp.float32)


def dot_rows(left, right):
    return lax.dot_general(
        left, right, (((0,), (0,)), ((), ())), preferred_element_type=jnp.float32
    )


def dot_cols(left, right):
    return lax.dot_general(
        left, right, (((1,), (1,)), ((), ())), preferred_element_type=jnp.float32
    )


def rms_forward(values, gain_vec):
    inv_rms = lax.rsqrt(jnp.mean(values * values, axis=-1, keepdims=True) + EPS)
    unit_rows = values * inv_rms
    return (unit_rows * gain_vec, unit_rows, inv_rms)


def rms_backward(grad_out, unit_rows, inv_rms, gain_vec):
    scaled = grad_out * gain_vec
    return inv_rms * (scaled - unit_rows * jnp.mean(scaled * unit_rows, axis=-1, keepdims=True))


def doc_layout(lengths, places):
    doc_ends = jnp.cumsum(lengths)
    starts = doc_ends - lengths
    owners = jnp.sum((places[:, None] >= doc_ends[None, :]).astype(jnp.int32), axis=1)
    member = owners[:, None] == jnp.arange(lengths.shape[0], dtype=jnp.int32)[None, :]
    inner_pos = places - jnp.sum(jnp.where(member, starts[None, :], 0), axis=1)
    return (owners, inner_pos)


def rotate(values, inner_pos, direction):
    half_dim = values.shape[-1] // 2
    frequency = ROPE_BASE ** (-jnp.arange(half_dim, dtype=jnp.float32) / half_dim)
    angles = inner_pos.astype(jnp.float32)[..., None] * frequency
    for padding_axis in range(values.ndim - 1 - angles.ndim + 1):
        angles = angles[..., None, :]
    cosine = jnp.cos(angles)
    sine_part = jnp.sin(angles) * direction
    front_half = values[..., :half_dim]
    back_half = values[..., half_dim:]
    return jnp.concatenate(
        [front_half * cosine - back_half * sine_part, back_half * cosine + front_half * sine_part],
        axis=-1,
    )


def key_scores(query_rows, key_piece, query_owner, query_place, lengths):
    count = key_piece.shape[1]
    key_places = jnp.arange(count, dtype=jnp.int32)

    def owner_rows(lengths_row):
        return doc_layout(lengths_row, key_places)[0]

    key_owner = jax.vmap(owner_rows)(lengths)
    scores = jnp.einsum(
        "rqd,rkd->rqk", query_rows, key_piece[..., :HD], preferred_element_type=jnp.float32
    ) * HD ** (-0.5)
    allowed = (query_owner[:, :, None] == key_owner[:, None, :]) & (
        key_places[None, None, :] <= query_place[None, :, None]
    )
    return (jnp.where(allowed, scores, NEG_FILL), allowed)


def forward_fold(carry, key_piece, query_rows, query_owner, query_place, lengths):
    row_peak, row_total, context = carry
    scores, allowed = key_scores(query_rows, key_piece, query_owner, query_place, lengths)
    new_peak = jnp.maximum(row_peak, jnp.max(scores, axis=-1))
    expo_vals = jnp.where(allowed, jnp.exp(scores - new_peak[..., None]), 0.0)
    row_total = jnp.sum(expo_vals, axis=-1)
    context = jnp.einsum(
        "rqk,rkd->rqd",
        expo_vals.astype(jnp.bfloat16),
        key_piece[..., HD:],
        preferred_element_type=jnp.float32,
    )
    return (new_peak, row_total, context)


def backward_fold(
    key_piece, query_rows, query_owner, query_place, lengths, log_total, context_rows, row_delta
):
    scores, allowed = key_scores(query_rows, key_piece, query_owner, query_place, lengths)
    probs = jnp.where(allowed, jnp.exp(scores - log_total[..., None]), 0.0)
    dprobs = jnp.einsum(
        "rqd,rkd->rqk", context_rows, key_piece[..., HD:], preferred_element_type=jnp.float32
    )
    dscores = (probs * (dprobs - row_delta[..., None])).astype(jnp.bfloat16)
    dquery = jnp.einsum(
        "rqk,rkd->rqd", dscores, key_piece[..., :HD], preferred_element_type=jnp.float32
    )
    dkeys = jnp.einsum(
        "rqk,rqd->rkd", dscores, query_rows, preferred_element_type=jnp.float32
    ) * HD ** (-0.5)
    dvalues = jnp.einsum(
        "rqk,rqd->rkd", probs.astype(jnp.bfloat16), context_rows, preferred_element_type=jnp.float32
    )
    update = jnp.concatenate([dkeys, dvalues], axis=-1)
    return (dquery, update)


def key_backward(kv_delta, inner_pos):
    turned = rotate(kv_delta[..., :HD], inner_pos, -1.0)
    return jnp.concatenate([turned, kv_delta[..., HD:]], axis=-1).astype(jnp.bfloat16)


def shards(
    layer_in,
    attn_gain,
    query_down,
    latent_gain,
    query_up,
    key_value,
    attn_out,
    ffn_gain,
    gate_proj,
    up_proj,
    down_proj,
    out_grad,
    doc_lengths,
):
    row_count, row_tokens, model_dim = layer_in.shape
    shard_index = lax.axis_index("seq")
    local_heads = query_up.shape[1] // HD
    tokens = row_count * row_tokens
    query_count = local_heads * row_tokens
    places = shard_index * row_tokens + jnp.arange(row_tokens, dtype=jnp.int32)

    def layout_row(lengths_row):
        return doc_layout(lengths_row, places)

    owners, inner_pos = jax.vmap(layout_row)(doc_lengths)
    stream = layer_in.astype(jnp.float32).reshape(tokens, model_dim)
    normed_full, unit_first, inv_first = rms_forward(stream, attn_gain)
    normed = normed_full.astype(jnp.bfloat16)
    latent = matmul(normed, query_down)
    latent_full, unit_latent, inv_latent = rms_forward(latent, latent_gain)
    latent_norm = latent_full.astype(jnp.bfloat16)
    raw_query = matmul(latent_norm, query_up).reshape(row_count, row_tokens, local_heads, HD)
    queries = rotate(raw_query, inner_pos, 1.0).astype(jnp.bfloat16)
    query_rows = queries.transpose(0, 2, 1, 3).reshape(row_count, query_count, HD)
    query_owner = jnp.tile(owners, (1, local_heads))
    query_place = jnp.tile(places, local_heads)
    kv_proj = matmul(normed, key_value).reshape(row_count, row_tokens, 2 * HD)
    key_part = rotate(kv_proj[..., :HD], inner_pos, 1.0)
    kv_shard = jnp.concatenate([key_part, kv_proj[..., HD:]], axis=-1).astype(jnp.bfloat16)
    start_carry = (
        jnp.full((row_count, query_count), NEG_FILL, jnp.float32),
        jnp.zeros((row_count, query_count), jnp.float32),
        jnp.zeros((row_count, query_count, HD), jnp.float32),
    )
    row_peak, row_total, context = forward_fold(
        start_carry,
        lax.all_gather(kv_shard, "seq", axis=1, tiled=True),
        query_rows,
        query_owner,
        query_place,
        doc_lengths,
    )
    context = context / row_total[..., None]
    log_total = row_peak + jnp.log(row_total)
    context_low = context.astype(jnp.bfloat16)
    context_flat = (
        context_low.reshape(row_count, local_heads, row_tokens, HD)
        .transpose(0, 2, 1, 3)
        .reshape(tokens, local_heads * HD)
    )
    attn_total = lax.psum(matmul(context_flat, attn_out), "tp")
    middle = stream + attn_total
    second_full, unit_second, inv_second = rms_forward(middle, ffn_gain)
    second_norm = second_full.astype(jnp.bfloat16)
    gate_act = matmul(second_norm, gate_proj)
    up_act = matmul(second_norm, up_proj)
    sigmoid_gate = jax.nn.sigmoid(gate_act)
    swish_gate = gate_act * sigmoid_gate
    hidden = (swish_gate * up_act).astype(jnp.bfloat16)
    ffn_total = lax.psum(matmul(hidden, down_proj), "tp")
    layer_out = (middle + ffn_total).astype(jnp.bfloat16).reshape(row_count, row_tokens, model_dim)
    grad_low = out_grad.reshape(tokens, model_dim)
    grad_full = grad_low.astype(jnp.float32)
    down_grad = dot_rows(hidden, grad_low)
    dhidden = dot_cols(grad_low, down_proj)
    gate_delta = (dhidden * up_act * sigmoid_gate * (1.0 + gate_act * (1.0 - sigmoid_gate))).astype(
        jnp.bfloat16
    )
    up_delta = (dhidden * swish_gate).astype(jnp.bfloat16)
    gate_grad = dot_rows(second_norm, gate_delta)
    upproj_grad = dot_rows(second_norm, up_delta)
    second_delta = lax.psum(dot_cols(gate_delta, gate_proj) + dot_cols(up_delta, up_proj), "tp")
    middle_delta = grad_full + rms_backward(second_delta, unit_second, inv_second, ffn_gain)
    middle_low = middle_delta.astype(jnp.bfloat16)
    mixer_grad = dot_rows(context_flat, middle_low)
    column_grads = (
        lax.psum_scatter(mixer_grad, "seq", scatter_dimension=1, tiled=True),
        lax.psum_scatter(down_grad, "seq", scatter_dimension=1, tiled=True),
    )
    context_delta = dot_cols(middle_low, attn_out).astype(jnp.bfloat16)
    context_rows = (
        context_delta.reshape(row_count, row_tokens, local_heads, HD)
        .transpose(0, 2, 1, 3)
        .reshape(row_count, query_count, HD)
    )
    row_delta = jnp.sum(context_rows.astype(jnp.float32) * context, axis=-1)
    dquery, key_deltas = backward_fold(
        lax.all_gather(kv_shard, "seq", axis=1, tiled=True),
        query_rows,
        query_owner,
        query_place,
        doc_lengths,
        log_total,
        context_rows,
        row_delta,
    )
    kv_part = lax.psum_scatter(key_deltas, "seq", scatter_dimension=1, tiled=True)
    dquery = dquery * HD ** (-0.5)
    query_delta = dquery.reshape(row_count, local_heads, row_tokens, HD).transpose(0, 2, 1, 3)
    query_low = (
        rotate(query_delta, inner_pos, -1.0).astype(jnp.bfloat16).reshape(tokens, local_heads * HD)
    )
    expand_grad = dot_rows(latent_norm, query_low)
    latent_part = dot_cols(query_low, query_up)
    latent_delta, kv_summed = lax.psum((latent_part, kv_part), "tp")
    kv_low = key_backward(kv_summed, inner_pos).reshape(tokens, 2 * HD)
    latent_back = rms_backward(latent_delta, unit_latent, inv_latent, latent_gain)
    latent_low = latent_back.astype(jnp.bfloat16)
    normed_delta = dot_cols(latent_low, query_down) + dot_cols(kv_low, key_value)
    input_grad = (
        (middle_delta + rms_backward(normed_delta, unit_first, inv_first, attn_gain))
        .astype(jnp.bfloat16)
        .reshape(row_count, row_tokens, model_dim)
    )
    gain_first = jnp.sum(normed_delta * unit_first, axis=0)
    gain_latent = jnp.sum(latent_delta * unit_latent, axis=0)
    gain_second = jnp.sum(second_delta * unit_second, axis=0)
    compress_grad = dot_rows(normed, latent_low)
    shared_grad = dot_rows(normed, kv_low)
    row_grads = (
        lax.psum_scatter(gain_first, "seq", scatter_dimension=0, tiled=True),
        lax.psum_scatter(compress_grad, "seq", scatter_dimension=0, tiled=True),
        lax.psum_scatter(gain_latent, "seq", scatter_dimension=0, tiled=True),
        lax.psum_scatter(expand_grad, "seq", scatter_dimension=0, tiled=True),
        lax.psum_scatter(shared_grad, "seq", scatter_dimension=0, tiled=True),
        lax.psum_scatter(gain_second, "seq", scatter_dimension=0, tiled=True),
        lax.psum_scatter(gate_grad, "seq", scatter_dimension=0, tiled=True),
        lax.psum_scatter(upproj_grad, "seq", scatter_dimension=0, tiled=True),
    )
    return (
        layer_out,
        input_grad,
        row_grads[0],
        row_grads[1],
        row_grads[2],
        row_grads[3],
        row_grads[4],
        column_grads[0],
        row_grads[5],
        row_grads[6],
        row_grads[7],
        column_grads[1],
    )


def solution(mesh):
    return jax.shard_map(
        shards,
        mesh=mesh,
        in_specs=(
            P(None, "seq", None),
            P(),
            P(),
            P(),
            P(None, "tp"),
            P(),
            P("tp", None),
            P(),
            P(None, "tp"),
            P(None, "tp"),
            P("tp", None),
            P(None, "seq", None),
            P(),
        ),
        out_specs=(
            P(None, "seq", None),
            P(None, "seq", None),
            P("seq"),
            P("seq", None),
            P("seq"),
            P("seq", "tp"),
            P("seq", None),
            P("tp", "seq"),
            P("seq"),
            P("seq", "tp"),
            P("seq", "tp"),
            P("tp", "seq"),
        ),
        check_vma=False,
    )
```

profile of v0, /device:TPU:0, one launch (start us, length us, event | category | flops | bytes accessed | tf_op | source)
XLA Modules:
  0.0 1362.6 jit_solution(8796911887741906710)
XLA Ops:
  9.1 2.1 fusion.20
  11.2 2.9 fusion.24
  14.2 1.8 fusion.45
  17.1 2.3 fusion.13
  19.8 2.4 multiply_reduce_fusion.6
  23.6 2.6 fusion.63
  26.2 3.5 reshape.210
  29.7 2.1 subtract_convert_fusion.1
  33.6 2.7 iota_compare_fusion
  36.3 20.2 %all-gather.2.cloned.1.call-done = bf16[2,2048,512]{2,1,0:T(8,128)(2,1)} async-done(((bf16[2,256,512]{2,1,0:T(8,128)(2,1)}), bf16[2,2048,512]{2,1,0:T(8,128)(2,1)}) %all-gather.2.cloned.1.call-update) | async-done | bytes 4194320 | tf_op jit(solution)/shard_map/all_gather | solution.py:170
  56.5 7.5 fusion.64
  64.6 6.1 fusion
  70.8 8.6 fusion.40
  79.4 2.2 copy.49
  82.8 4.4 fusion.65
  87.3 155.1 %all-reduce.9.cloned.1.call-done = f32[512,2048]{1,0:T(8,128)} async-done(((f32[512,2048]{1,0:T(8,128)}), f32[512,2048]{1,0:T(8,128)}) %all-reduce.9.cloned.1.call-update) | async-done | bytes 4194320 | tf_op jit(solution)/shard_map/psum | solution.py:184
  242.3 3.5 multiply_reduce_fusion.2
  246.3 10.1 fusion.67
  256.5 5.0 fusion.66
  261.5 8.1 multiply_convert_fusion.2
  269.6 4.9 fusion.69
  274.6 5.1 convolution_add_fusion.1
  280.4 153.5 %all-reduce.11.cloned.1.call-done = f32[512,2048]{1,0:T(8,128)} async-done(((f32[512,2048]{1,0:T(8,128)}), f32[512,2048]{1,0:T(8,128)}) %all-reduce.11.cloned.1.call-update) | async-done | bytes 4194320 | tf_op jit(solution)/shard_map/psum | solution.py:205
  433.9 4.6 multiply_reduce_fusion
  438.5 1.3 copy-done.10
  439.8 2.8 multiply_add_fusion
  442.6 2.0 copy-done.3
  444.6 3.3 convolution_convert_fusion
  447.9 2.0 reshape.216
  450.1 2.4 multiply_reduce_fusion.5
  452.5 12.0 fusion.3
  464.5 13.9 %multiply_convert_fusion = bf16[2,1024,2048]{2,1,0:T(8,128)(2,1)} fusion(f32[2,1024,2048]{2,1,0:T(8,128)} %copy-done.9, f32[2,1024]{1,0:T(2,128)S(1)} %multiply_reduce_fusion.5, f32[2,1024]{1,0:T(2,128)S(1)} %log_add_fusion, s32[2,2048]{1,0:T(2,128)S(1)} %convert_reduce_fusion, s32[2,1024]{1,0:T(2,128)S(1)} %bitcast.132, ...), kind=kOutput, calls=%fused_computation | convolution fusion | flops 2176843776 | bytes 30449664 | tf_op jit(solution)/shard_map/rqd,rkd->rqk/dot_general | solution.py:101
  478.4 6.9 convolution_multiply_fusion
  485.4 4.6 pad_maximum_fusion
  490.0 1.3 copy-done.52
  491.3 8.2 fusion.68
  499.6 7.2 fusion.34
  506.8 1.4 copy.66
  509.7 2.6 fusion.70
  512.3 48.1 %reduce-scatter.9.cloned.1.call-done = f32[2,256,512]{2,1,0:T(8,128)} async-done(((f32[2,2048,512]{2,1,0:T(8,128)}), f32[2,256,512]{2,1,0:T(8,128)}) %reduce-scatter.9.cloned.1.call-update) | async-done | bytes 1048592 | tf_op jit(solution)/shard_map/reduce_scatter | solution.py:230
  560.5 5.1 fusion.62
  566.8 8.0 fusion.37
  576.1 9.0 fusion.75
  585.2 1.3 copy-done.56
  586.5 7.7 fusion.74
  594.3 1.3 copy-done.54
  595.6 7.8 fusion.73
  603.4 217.7 %all-reduce.13.cloned.1.call-done = (f32[512,2048]{1,0:T(8,128)}, f32[512,1024]{1,0:T(8,128)}, f32[2,256,512]{2,1,0:T(8,128)}) async-done(((f32[512,2048]{1,0:T(8,128)}, f32[512,1024]{1,0:T(8,128)}, f32[2,256,512]{2,1,0:T(8,128)}), (f32[512,2048]{1,0:T(8,128)}, f32[512,1024]{1,0:T(8,128)}, f32[2,256,512]{2,1,0:T(8,128)})) %all-reduce.13.cloned.1.call-update) | async-done | bytes 7340048 | tf_op jit(solution)/shard_map/psum | solution.py:193
  822.2 2.2 fusion.53
  825.0 4.9 fusion.56
  830.3 4.0 multiply_reduce_fusion.3
  835.4 5.7 fusion.72
  843.7 4.7 fusion.71
  848.5 3.8 fusion.19
  852.3 24.3 %all-reduce.3 = (f32[2048]{0:T(1024)S(1)}, f32[1024]{0:T(1024)S(1)}, f32[2048]{0:T(1024)S(1)}) all-reduce(f32[2048]{0:T(1024)S(1)} %get-tuple-element.14, f32[1024]{0:T(1024)S(1)} %copy-done.42, f32[2048]{0:T(1024)S(1)} %get-tuple-element.12), channel_id=3, replica_groups=mesh['seq'=8,'tp'=4] {'seq'}, use_global_device_ids=true, to_apply=%region_20.21.clone | all-reduce | flops 5120 | bytes 40960
  878.4 5.6 add_convert_fusion
  884.0 2.2 copy-done.16
  886.2 2.4 fusion.18
  888.6 62.4 %reduce-scatter.17.cloned.1.call-done = f32[1024,256]{1,0:T(8,128)} async-done(((f32[1024,2048]{1,0:T(8,128)}), f32[1024,256]{1,0:T(8,128)}) %reduce-scatter.17.cloned.1.call-update) | async-done | bytes 1048592 | tf_op jit(solution)/shard_map/reduce_scatter | solution.py:210
  951.0 91.3 %reduce-scatter.23.cloned.1.call-done = f32[1408,256]{1,0:T(8,128)} async-done(((f32[1408,2048]{1,0:T(8,128)}), f32[1408,256]{1,0:T(8,128)}) %reduce-scatter.23.cloned.1.call-update) | async-done | bytes 1441808 | tf_op jit(solution)/shard_map/reduce_scatter | solution.py:211
  1042.3 91.3 %reduce-scatter.21.cloned.1.call-done = f32[256,1408]{1,0:T(8,128)} async-done(((f32[2048,1408]{1,0:T(8,128)}), f32[256,1408]{1,0:T(8,128)}) %reduce-scatter.21.cloned.1.call-update) | async-done | bytes 1441808 | tf_op jit(solution)/shard_map/reduce_scatter | solution.py:261
  1133.6 91.1 %reduce-scatter.19.cloned.1.call-done = f32[256,1408]{1,0:T(8,128)} async-done(((f32[2048,1408]{1,0:T(8,128)}), f32[256,1408]{1,0:T(8,128)}) %reduce-scatter.19.cloned.1.call-update) | async-done | bytes 1441808 | tf_op jit(solution)/shard_map/reduce_scatter | solution.py:260
  1224.7 55.6 %reduce-scatter.15.cloned.1.call-done = f32[256,512]{1,0:T(8,128)} async-done(((f32[2048,512]{1,0:T(8,128)}), f32[256,512]{1,0:T(8,128)}) %reduce-scatter.15.cloned.1.call-update) | async-done | bytes 524304 | tf_op jit(solution)/shard_map/reduce_scatter | solution.py:258
  1280.4 75.2 %reduce-scatter.11.cloned.1.call-done = f32[256,1024]{1,0:T(8,128)} async-done(((f32[2048,1024]{1,0:T(8,128)}), f32[256,1024]{1,0:T(8,128)}) %reduce-scatter.11.cloned.1.call-update) | async-done | bytes 1048592 | tf_op jit(solution)/shard_map/reduce_scatter | solution.py:255
  (185 shorter events, 20.4 us)
Async XLA Ops:
  7.2 4.0 copy-start
  7.2 49.3 %all-gather.2.cloned.1.call-start = ((), (), s32[]{:S(2)}) async-start(), calls=%async_computation.8 | async-start | bytes 4718592 | tf_op jit(solution)/shard_map/all_gather | solution.py:170
  7.3 6.9 copy-start.43
  9.1 5.1 copy-start.40
  11.2 5.8 copy-start.33
  16.0 13.7 %copy-start.20 = (f32[2,256,128]{2,1,0:T(8,128)}, f32[2,256,128]{2,1,0:T(8,128)S(1)}, u32[]{:S(2)}) copy-start(f32[2,256,128]{2,1,0:T(8,128)S(1)} %get-tuple-element.41) | copy-start | bytes 786436
  16.9 225.4 %all-reduce.9.cloned.1.call-start = ((), (), s32[]{:S(2)}) async-start(), calls=%async_computation.9 | async-start | bytes 8388608 | tf_op jit(solution)/shard_map/psum | solution.py:184
  17.0 2.8 copy-start.47
  17.0 5.3 copy-start.37
  19.8 2.5 copy-start.11
  19.8 3.7 copy-start.28
  19.8 3.7 copy-start.49
  56.5 8.1 copy-start.14
  64.0 6.7 copy-start.9
  79.4 3.4 copy-start.45
  87.2 158.6 %copy-start.30 = (f32[2048]{0:T(1024)S(1)}, f32[2048]{0:T(1024)}, u32[]{:S(2)}) copy-start(f32[2048]{0:T(1024)} %param.20) | copy-start | bytes 24580
  87.2 346.6 %all-reduce.11.cloned.1.call-start = ((), (), s32[]{:S(2)}) async-start(), calls=%async_computation.10 | async-start | bytes 8388608 | tf_op jit(solution)/shard_map/psum | solution.py:205
  245.8 10.6 copy-start.1
  245.9 10.6 slice-start
  246.3 10.1 copy-start.22
  246.3 10.1 slice-start.1
  246.3 15.2 %slice-start.4 = ((s8[5767168]{0:T(1024)(128)(4,1)}), s8[4194304]{0:T(1024)(128)(4,1)S(1)}, s32[]{:S(2)}) async-start(s8[5767168]{0:T(1024)(128)(4,1)} %bitcast.141), calls=%async_computation.24 | async-start | bytes 8388608
  256.4 5.1 copy-start.23
  256.4 5.0 slice-start.5
  256.5 18.1 %slice-start.2 = ((s8[5767168]{0:T(1024)(128)(4,1)}), s8[4194304]{0:T(1024)(128)(4,1)S(1)}, s32[]{:S(2)}) async-start(s8[5767168]{0:T(1024)(128)(4,1)} %bitcast.139), calls=%async_computation.22 | async-start | bytes 8388608
  261.5 13.1 slice-start.3
  269.6 5.0 copy-start.55
  279.7 280.7 %reduce-scatter.9.cloned.1.call-start = ((), (), s32[]{:S(2)}) async-start(), calls=%async_computation.11 | async-start | bytes 9437184 | tf_op jit(solution)/shard_map/reduce_scatter | solution.py:230
  433.9 4.6 copy-start.2
  433.9 5.9 copy-start.10
  439.8 4.8 copy-start.46
  442.6 2.0 copy-start.3
  450.0 2.6 copy-start.15
  464.5 13.9 %copy-start.25 = (bf16[2,4,256,256]{3,2,1,0:T(8,128)(2,1)S(1)}, bf16[2,4,256,256]{3,2,1,0:T(8,128)(2,1)}, u32[]{:S(2)}) copy-start(bf16[2,4,256,256]{3,2,1,0:T(8,128)(2,1)} %copy.48) | copy-start | bytes 3145732
  478.4 7.0 copy-start.17
  490.0 331.1 %all-reduce.13.cloned.1.call-start = ((), (), s32[]{:S(2)}) async-start(), calls=%async_computation.19 | async-start | bytes 14680064 | tf_op jit(solution)/shard_map/psum | solution.py:193
  491.3 8.3 copy-start.48
  506.7 1.4 copy-start.21
  506.8 1.4 copy-start.24
  508.1 1.6 copy-start.50
  512.3 48.2 %copy-start.29 = (f32[1024]{0:T(1024)S(1)}, f32[1024]{0:T(1024)}, u32[]{:S(2)}) copy-start(f32[1024]{0:T(1024)} %param.16) | copy-start | bytes 12292
  512.3 48.2 %copy-start.32 = (f32[512]{0:T(512)S(1)}, f32[512]{0:T(512)}, u32[]{:S(2)}) copy-start(f32[512]{0:T(512)} %copy-done.31) | copy-start | bytes 6148
  560.4 328.2 %reduce-scatter.13.cloned.1.call-start = ((), (), s32[]{:S(2)}) async-start(), calls=%async_computation.13 | async-start | bytes 4718592 | tf_op jit(solution)/shard_map/reduce_scatter | solution.py:257
  565.6 385.5 %reduce-scatter.17.cloned.1.call-start = ((), (), s32[]{:S(2)}) async-start(), calls=%async_computation.15 | async-start | bytes 9437184 | tf_op jit(solution)/shard_map/reduce_scatter | solution.py:210
  574.8 1.4 copy-start.53
  574.8 467.5 %reduce-scatter.23.cloned.1.call-start = ((), (), s32[]{:S(2)}) async-start(), calls=%async_computation.18 | async-start | bytes 12976128 | tf_op jit(solution)/shard_map/reduce_scatter | solution.py:211
  585.1 548.5 %reduce-scatter.21.cloned.1.call-start = ((), (), s32[]{:S(2)}) async-start(), calls=%async_computation.17 | async-start | bytes 12976128 | tf_op jit(solution)/shard_map/reduce_scatter | solution.py:261
  594.2 630.5 %reduce-scatter.19.cloned.1.call-start = ((), (), s32[]{:S(2)}) async-start(), calls=%async_computation.16 | async-start | bytes 12976128 | tf_op jit(solution)/shard_map/reduce_scatter | solution.py:260
  603.3 218.8 %copy-start.41 = (f32[2,256]{1,0:T(2,128)S(1)}, f32[2,256]{1,0:T(2,128)}, u32[]{:S(2)}) copy-start(f32[2,256]{1,0:T(2,128)} %copy-done.40) | copy-start | bytes 6148
  603.3 218.8 %copy-start.44 = (f32[128]{0:T(128)S(1)}, f32[128]{0:T(128)}, u32[]{:S(2)}) copy-start(f32[128]{0:T(128)} %copy-done.43) | copy-start | bytes 1540
  603.4 677.0 %reduce-scatter.15.cloned.1.call-start = ((), (), s32[]{:S(2)}) async-start(), calls=%async_computation.14 | async-start | bytes 4718592 | tf_op jit(solution)/shard_map/reduce_scatter | solution.py:258
  830.0 525.6 %reduce-scatter.11.cloned.1.call-start = ((), (), s32[]{:S(2)}) async-start(), calls=%async_computation.12 | async-start | bytes 9437184 | tf_op jit(solution)/shard_map/reduce_scatter | solution.py:255
  830.2 4.0 copy-start.8
  830.2 4.3 copy-start.13
  830.3 5.2 copy-start.12
  843.7 4.8 copy-start.5
  843.7 4.8 copy-start.27
  843.7 4.8 copy-start.34
  843.7 4.8 copy-start.38
  848.5 3.8 copy-start.42
  848.5 35.5 %copy-start.39 = (f32[1,2,2,128]{3,1,2,0:T(2,128)S(1)}, f32[1,2,2,128]{3,1,2,0:T(2,128)}, u32[]{:S(2)}) copy-start(f32[1,2,2,128]{3,1,2,0:T(2,128)} %copy-done.37) | copy-start | bytes 6148
  878.4 5.6 copy-start.4
  878.4 5.6 copy-start.6
  878.4 7.8 copy-start.16
  (11 other events, 11.5 us)
Sparse Core Ops, SparseCore 0:
  17.1 39.4 all-gather.1
  87.3 154.9 all-reduce.8
  279.8 153.9 all-reduce.10
  490.1 70.2 reduce-scatter.8
  563.6 257.4 all-reduce.12
  825.2 50.4 reduce-scatter.12
  879.8 71.2 reduce-scatter.16
  955.5 86.7 reduce-scatter.22
  1046.8 86.7 reduce-scatter.20
  1137.9 86.7 reduce-scatter.18
  1229.0 51.2 reduce-scatter.14
  1284.3 71.2 reduce-scatter.10
where the time goes:
time: 1370 us; the launch traced here: 1360 us
  waiting for transfers between devices  1060 us (77%)
  matrix products  172 us (13%)
  other arithmetic  54.6 us (4%)
  local copies, waits for them, and re-layouts  32.3 us (2%)
  blocking collectives  24.3 us (2%)
  between operations  16.5 us (1%)
    psum x1, waiting for transfers between devices, shards(): ffn_total = lax.psum(matmul(hidden, down_proj), 'tp')  218 us
    psum x1, waiting for transfers between devices, shards(): attn_total = lax.psum(matmul(context_flat, attn_out), 'tp')  155 us
    psum x1, waiting for transfers between devices, shards(): lax.psum(dot_cols(gate_delta, gate_proj) + dot_cols(up_delta, up_proj), '...  153 us
    reduce_scatter x1, waiting for transfers between devices, shards(): lax.psum_scatter(upproj_grad, 'seq', scatter_dimension=0, tiled=True)  91.3 us
    reduce_scatter x1, waiting for transfers between devices, shards(): lax.psum_scatter(down_grad, 'seq', scatter_dimension=1, tiled=True)  91.3 us
    reduce_scatter x1, waiting for transfers between devices, shards(): lax.psum_scatter(gate_grad, 'seq', scatter_dimension=0, tiled=True)  91.1 us
    reduce_scatter x1, waiting for transfers between devices, shards(): lax.psum_scatter(compress_grad, 'seq', scatter_dimension=0, tiled=True)  75.2 us
    reduce_scatter x1, waiting for transfers between devices, shards(): lax.psum_scatter(mixer_grad, 'seq', scatter_dimension=1, tiled=True)  62.4 us
  transfers between devices with their start and end apart: 12, of which 11 were waited for; matrix products, arithmetic and copies ran while one was open for 8% of the time, Pallas kernels for 0%

commit v1 on v0

--- a/solution.py
+++ b/solution.py
@@ -181,7 +181,7 @@
         .transpose(0, 2, 1, 3)
         .reshape(tokens, local_heads * HD)
     )
-    attn_total = lax.psum(matmul(context_flat, attn_out), "tp")
+    attn_total = jnp.sum(lax.all_gather(matmul(context_flat, attn_out), "tp"), axis=0)
     middle = stream + attn_total
     second_full, unit_second, inv_second = rms_forward(middle, ffn_gain)
     second_norm = second_full.astype(jnp.bfloat16)

time: 1370 us -> 1510 us (1.10)
  waiting for transfers between devices: 1060 us -> 1190 us
    all_gather x0 -> x1, waiting for transfers between devices: none -> 287 us  [shards(): lax.all_gather(matmul(context_flat, attn_out), 'tp')]
    psum x1 -> x0, waiting for transfers between devices: 155 us -> none  [shards(): attn_total = lax.psum(matmul(context_flat, attn_out), 'tp')]
where the time goes in v1:
time: 1510 us; the launch traced here: 1500 us
  waiting for transfers between devices  1190 us (79%)
  matrix products  171 us (11%)
  other arithmetic  68.5 us (5%)
  local copies, waits for them, and re-layouts  31.9 us (2%)
  blocking collectives  24.1 us (2%)
  between operations  16.5 us (1%)
    all_gather x1, waiting for transfers between devices, shards(): lax.all_gather(matmul(context_flat, attn_out), 'tp')  287 us
    psum x1, waiting for transfers between devices, shards(): ffn_total = lax.psum(matmul(hidden, down_proj), 'tp')  217 us
    psum x1, waiting for transfers between devices, shards(): lax.psum(dot_cols(gate_delta, gate_proj) + dot_cols(up_delta, up_proj), '...  153 us
    reduce_scatter x1, waiting for transfers between devices, shards(): lax.psum_scatter(upproj_grad, 'seq', scatter_dimension=0, tiled=True)  90.9 us
    reduce_scatter x1, waiting for transfers between devices, shards(): lax.psum_scatter(down_grad, 'seq', scatter_dimension=1, tiled=True)  90.9 us
    reduce_scatter x1, waiting for transfers between devices, shards(): lax.psum_scatter(gate_grad, 'seq', scatter_dimension=0, tiled=True)  90.7 us
    reduce_scatter x1, waiting for transfers between devices, shards(): lax.psum_scatter(compress_grad, 'seq', scatter_dimension=0, tiled=True)  75.6 us
    reduce_scatter x1, waiting for transfers between devices, shards(): lax.psum_scatter(mixer_grad, 'seq', scatter_dimension=1, tiled=True)  62.8 us
  transfers between devices with their start and end apart: 12, of which 11 were waited for; matrix products, arithmetic and copies ran while one was open for 8% of the time, Pallas kernels for 0%

profile of v1, /device:TPU:0, one launch (start us, length us, event | category | flops | bytes accessed | tf_op | source)
XLA Modules:
  0.0 1504.4 jit_solution(8583992302834394761)
XLA Ops:
  9.1 2.1 fusion.20
  11.2 2.9 fusion.26
  14.2 1.8 fusion.47
  17.1 2.3 fusion.13
  19.8 2.4 multiply_reduce_fusion.5
  22.3 1.3 copy-done.7
  23.6 2.6 fusion.65
  26.2 3.7 reshape.220
  30.0 2.1 subtract_convert_fusion.1
  33.8 2.7 iota_compare_fusion
  36.5 20.0 %all-gather.4.cloned.1.call-done = bf16[2,2048,512]{2,1,0:T(8,128)(2,1)} async-done(((bf16[2,256,512]{2,1,0:T(8,128)(2,1)}), bf16[2,2048,512]{2,1,0:T(8,128)(2,1)}) %all-gather.4.cloned.1.call-update) | async-done | bytes 4194320 | tf_op jit(solution)/shard_map/all_gather | solution.py:170
  56.5 7.5 fusion.66
  64.7 6.1 fusion
  70.8 8.2 fusion.42
  79.0 2.2 copy.49
  82.5 4.4 fusion.67
  86.9 286.9 %all-gather.6.cloned.1.call-done = f32[2048,2048]{1,0:T(8,128)} async-done(((f32[512,2048]{1,0:T(8,128)}), f32[2048,2048]{1,0:T(8,128)}) %all-gather.6.cloned.1.call-update) | async-done | bytes 16777232 | tf_op jit(solution)/shard_map/all_gather | solution.py:184
  373.8 10.2 reduce_sum.147
  383.9 3.6 fusion.24
  389.3 8.7 fusion.69
  398.2 4.9 fusion.68
  403.1 8.2 multiply_convert_fusion.2
  411.3 4.9 fusion.71
  416.3 5.1 convolution_add_fusion.1
  422.2 152.6 %all-reduce.8.cloned.1.call-done = f32[512,2048]{1,0:T(8,128)} async-done(((f32[512,2048]{1,0:T(8,128)}), f32[512,2048]{1,0:T(8,128)}) %all-reduce.8.cloned.1.call-update) | async-done | bytes 4194320 | tf_op jit(solution)/shard_map/psum | solution.py:205
  574.8 5.4 multiply_reduce_fusion
  580.7 1.2 copy-done.10
  581.9 3.4 multiply_add_fusion
  585.3 2.0 copy-done.6
  587.3 3.4 convolution_convert_fusion
  590.6 2.2 reshape.226
  593.0 2.4 multiply_reduce_fusion.4
  595.4 12.0 fusion.3
  607.5 13.8 multiply_convert_fusion
  621.3 6.9 convolution_multiply_fusion
  628.3 4.6 pad_maximum_fusion
  633.0 1.3 copy-done.51
  634.2 7.9 fusion.70
  642.2 7.2 fusion.36
  649.4 1.4 copy.67
  652.4 2.6 fusion.72
  655.0 48.4 %reduce-scatter.9.cloned.1.call-done = f32[2,256,512]{2,1,0:T(8,128)} async-done(((f32[2,2048,512]{2,1,0:T(8,128)}), f32[2,256,512]{2,1,0:T(8,128)}) %reduce-scatter.9.cloned.1.call-update) | async-done | bytes 1048592 | tf_op jit(solution)/shard_map/reduce_scatter | solution.py:230
  703.5 5.0 fusion.64
  709.7 8.1 fusion.39
  719.1 9.0 fusion.77
  728.2 1.3 copy-done.55
  729.4 7.9 fusion.76
  737.4 1.3 copy-done.53
  738.7 7.7 fusion.75
  746.5 217.4 %all-reduce.10.cloned.1.call-done = (f32[512,2048]{1,0:T(8,128)}, f32[512,1024]{1,0:T(8,128)}, f32[2,256,512]{2,1,0:T(8,128)}) async-done(((f32[512,2048]{1,0:T(8,128)}, f32[512,1024]{1,0:T(8,128)}, f32[2,256,512]{2,1,0:T(8,128)}), (f32[512,2048]{1,0:T(8,128)}, f32[512,1024]{1,0:T(8,128)}, f32[2,256,512]{2,1,0:T(8,128)})) %all-reduce.10.cloned.1.call-update) | async-done | bytes 7340048 | tf_op jit(solution)/shard_map/psum | solution.py:193
  964.9 2.2 fusion.55
  967.8 4.9 fusion.58
  973.1 4.1 multiply_reduce_fusion.2
  978.3 5.7 fusion.74
  986.6 4.8 fusion.73
  991.5 3.8 fusion.19
  995.2 24.1 %all-reduce.3 = (f32[2048]{0:T(1024)S(1)}, f32[1024]{0:T(1024)S(1)}, f32[2048]{0:T(1024)S(1)}) all-reduce(f32[2048]{0:T(1024)S(1)} %get-tuple-element.14, f32[1024]{0:T(1024)S(1)} %copy-done.41, f32[2048]{0:T(1024)S(1)} %get-tuple-element.12), channel_id=4, replica_groups=mesh['seq'=8,'tp'=4] {'seq'}, use_global_device_ids=true, to_apply=%region_20.21.clone | all-reduce | flops 5120 | bytes 40960
  1021.2 9.9 fusion.18
  1031.1 62.8 %reduce-scatter.17.cloned.1.call-done = f32[1024,256]{1,0:T(8,128)} async-done(((f32[1024,2048]{1,0:T(8,128)}), f32[1024,256]{1,0:T(8,128)}) %reduce-scatter.17.cloned.1.call-update) | async-done | bytes 1048592 | tf_op jit(solution)/shard_map/reduce_scatter | solution.py:210
  1093.9 90.9 %reduce-scatter.23.cloned.1.call-done = f32[1408,256]{1,0:T(8,128)} async-done(((f32[1408,2048]{1,0:T(8,128)}), f32[1408,256]{1,0:T(8,128)}) %reduce-scatter.23.cloned.1.call-update) | async-done | bytes 1441808 | tf_op jit(solution)/shard_map/reduce_scatter | solution.py:211
  1184.8 90.9 %reduce-scatter.21.cloned.1.call-done = f32[256,1408]{1,0:T(8,128)} async-done(((f32[2048,1408]{1,0:T(8,128)}), f32[256,1408]{1,0:T(8,128)}) %reduce-scatter.21.cloned.1.call-update) | async-done | bytes 1441808 | tf_op jit(solution)/shard_map/reduce_scatter | solution.py:261
  1275.7 90.7 %reduce-scatter.19.cloned.1.call-done = f32[256,1408]{1,0:T(8,128)} async-done(((f32[2048,1408]{1,0:T(8,128)}), f32[256,1408]{1,0:T(8,128)}) %reduce-scatter.19.cloned.1.call-update) | async-done | bytes 1441808 | tf_op jit(solution)/shard_map/reduce_scatter | solution.py:260
  1366.4 55.3 %reduce-scatter.15.cloned.1.call-done = f32[256,512]{1,0:T(8,128)} async-done(((f32[2048,512]{1,0:T(8,128)}), f32[256,512]{1,0:T(8,128)}) %reduce-scatter.15.cloned.1.call-update) | async-done | bytes 524304 | tf_op jit(solution)/shard_map/reduce_scatter | solution.py:258
  1421.7 75.6 %reduce-scatter.11.cloned.1.call-done = f32[256,1024]{1,0:T(8,128)} async-done(((f32[2048,1024]{1,0:T(8,128)}), f32[256,1024]{1,0:T(8,128)}) %reduce-scatter.11.cloned.1.call-update) | async-done | bytes 1048592 | tf_op jit(solution)/shard_map/reduce_scatter | solution.py:255
  (184 shorter events, 20.9 us)
Async XLA Ops:
  7.2 4.0 copy-start
  7.2 49.3 %all-gather.4.cloned.1.call-start = ((), (), s32[]{:S(2)}) async-start(), calls=%async_computation.8 | async-start | bytes 4718592 | tf_op jit(solution)/shard_map/all_gather | solution.py:170
  7.3 6.9 copy-start.42
  9.1 5.1 copy-start.39
  11.2 5.8 copy-start.32
  16.0 13.9 copy-start.19
  16.9 356.8 %all-gather.6.cloned.1.call-start = ((), (), s32[]{:S(2)}) async-start(), calls=%async_computation.18 | async-start | bytes 20971520 | tf_op jit(solution)/shard_map/all_gather | solution.py:184
  17.0 2.8 copy-start.46
  17.0 5.3 copy-start.36
  19.8 2.5 copy-start.11
  19.8 3.8 copy-start.27
  19.8 3.8 copy-start.48
  56.5 8.1 copy-start.14
  64.1 6.7 copy-start.9
  79.0 3.4 copy-start.44
  86.8 487.9 %all-reduce.8.cloned.1.call-start = ((), (), s32[]{:S(2)}) async-start(), calls=%async_computation.9 | async-start | bytes 8388608 | tf_op jit(solution)/shard_map/psum | solution.py:205
  383.9 4.1 copy-start.1
  383.9 4.7 copy-start.3
  383.9 4.7 copy-start.29
  388.7 9.4 slice-start
  389.3 8.8 copy-start.22
  389.3 8.8 slice-start.1
  389.3 13.8 slice-start.4
  398.1 5.0 copy-start.21
  398.1 5.0 slice-start.5
  398.1 18.1 %slice-start.2 = ((s8[5767168]{0:T(1024)(128)(4,1)}), s8[4194304]{0:T(1024)(128)(4,1)S(1)}, s32[]{:S(2)}) async-start(s8[5767168]{0:T(1024)(128)(4,1)} %bitcast.158), calls=%async_computation.22 | async-start | bytes 8388608
  403.1 13.2 slice-start.3
  411.3 5.0 copy-start.54
  421.5 281.9 %reduce-scatter.9.cloned.1.call-start = ((), (), s32[]{:S(2)}) async-start(), calls=%async_computation.10 | async-start | bytes 9437184 | tf_op jit(solution)/shard_map/reduce_scatter | solution.py:230
  574.8 5.4 copy-start.2
  574.8 5.9 copy-start.4
  574.8 7.1 copy-start.10
  581.9 5.4 copy-start.45
  585.3 2.0 copy-start.6
  592.9 2.6 copy-start.15
  607.5 13.8 copy-start.24
  621.3 7.0 copy-start.16
  632.9 1.4 copy-start.51
  632.9 330.9 %all-reduce.10.cloned.1.call-start = ((), (), s32[]{:S(2)}) async-start(), calls=%async_computation.19 | async-start | bytes 14680064 | tf_op jit(solution)/shard_map/psum | solution.py:193
  634.2 7.9 copy-start.47
  649.4 1.4 copy-start.20
  649.4 1.4 copy-start.23
  650.8 1.6 copy-start.49
  655.0 48.5 %copy-start.28 = (f32[1024]{0:T(1024)S(1)}, f32[1024]{0:T(1024)}, u32[]{:S(2)}) copy-start(f32[1024]{0:T(1024)} %param.16) | copy-start | bytes 12292
  655.0 48.5 %copy-start.31 = (f32[512]{0:T(512)S(1)}, f32[512]{0:T(512)}, u32[]{:S(2)}) copy-start(f32[512]{0:T(512)} %copy-done.30) | copy-start | bytes 6148
  703.4 327.7 %reduce-scatter.13.cloned.1.call-start = ((), (), s32[]{:S(2)}) async-start(), calls=%async_computation.12 | async-start | bytes 4718592 | tf_op jit(solution)/shard_map/reduce_scatter | solution.py:257
  708.5 385.4 %reduce-scatter.17.cloned.1.call-start = ((), (), s32[]{:S(2)}) async-start(), calls=%async_computation.14 | async-start | bytes 9437184 | tf_op jit(solution)/shard_map/reduce_scatter | solution.py:210
  717.8 467.0 %reduce-scatter.23.cloned.1.call-start = ((), (), s32[]{:S(2)}) async-start(), calls=%async_computation.17 | async-start | bytes 12976128 | tf_op jit(solution)/shard_map/reduce_scatter | solution.py:211
  728.1 547.6 %reduce-scatter.21.cloned.1.call-start = ((), (), s32[]{:S(2)}) async-start(), calls=%async_computation.16 | async-start | bytes 12976128 | tf_op jit(solution)/shard_map/reduce_scatter | solution.py:261
  737.3 1.4 copy-start.53
  737.3 629.1 %reduce-scatter.19.cloned.1.call-start = ((), (), s32[]{:S(2)}) async-start(), calls=%async_computation.15 | async-start | bytes 12976128 | tf_op jit(solution)/shard_map/reduce_scatter | solution.py:260
  746.4 218.5 %copy-start.40 = (f32[2,256]{1,0:T(2,128)S(1)}, f32[2,256]{1,0:T(2,128)}, u32[]{:S(2)}) copy-start(f32[2,256]{1,0:T(2,128)} %copy-done.39) | copy-start | bytes 6148
  746.4 218.5 %copy-start.43 = (f32[128]{0:T(128)S(1)}, f32[128]{0:T(128)}, u32[]{:S(2)}) copy-start(f32[128]{0:T(128)} %copy-done.42) | copy-start | bytes 1540
  746.4 675.3 %reduce-scatter.15.cloned.1.call-start = ((), (), s32[]{:S(2)}) async-start(), calls=%async_computation.13 | async-start | bytes 4718592 | tf_op jit(solution)/shard_map/reduce_scatter | solution.py:258
  972.8 524.5 %reduce-scatter.11.cloned.1.call-start = ((), (), s32[]{:S(2)}) async-start(), calls=%async_computation.11 | async-start | bytes 9437184 | tf_op jit(solution)/shard_map/reduce_scatter | solution.py:255
  973.1 4.1 copy-start.8
  973.1 4.4 copy-start.13
  973.1 5.2 copy-start.12
  986.6 4.8 copy-start.5
  986.6 4.8 copy-start.26
  986.6 4.8 copy-start.33
  986.6 4.8 copy-start.37
  991.4 3.8 copy-start.41
  991.4 29.8 %copy-start.38 = (f32[1,2,2,128]{3,1,2,0:T(2,128)S(1)}, f32[1,2,2,128]{3,1,2,0:T(2,128)}, u32[]{:S(2)}) copy-start(f32[1,2,2,128]{3,1,2,0:T(2,128)} %copy-done.36) | copy-start | bytes 6148
  (10 other events, 10.1 us)
Sparse Core Ops, SparseCore 0:
  17.1 39.3 all-gather.3
  87.0 286.7 all-gather.5
  421.6 153.1 all-reduce.7
  633.0 70.2 reduce-scatter.8
  706.4 257.4 all-reduce.9
  967.6 50.4 reduce-scatter.12
  1022.6 71.2 reduce-scatter.16
  1098.0 86.7 reduce-scatter.22
  1188.9 86.7 reduce-scatter.20
  1279.6 86.7 reduce-scatter.18
  1370.4 51.3 reduce-scatter.14
  1426.0 71.2 reduce-scatter.10
